TPU v7x, 32 devices: a whole 2x2x4 slice. The times are simulated.
32 devices in a mesh: group: 2 (over x), azim: 16 (over z, y, core).
Axes of the slice: x: 2, y: 2, z: 4, core: 2. Of those that a mesh axis runs over, the one named last changes fastest.
Arguments:
- field: bfloat16 [704, 8, 8, 640], P(('group', 'azim')), parts along dimension 0, may hold values from -6 to 6
- jacobian: bfloat16 [5, 8, 2, 320, 320], P(None, None, None, 'azim'), may hold values from -0.109375 to 0.109375
- coupling: int32 [16, 5], replicated, may hold values 0 or 1
Outputs:
- transferred: bfloat16 [704, 8, 8, 640], P(('group', 'azim')), parts along dimension 0
There are 2 independent parts, one for each index of `group`. A program takes and returns all parts, laid end to end along the dimension named above; an argument that names none is the same for every part. Nothing has to cross between parts.
All inputs are finite; a program needn't handle non-finite values.
Results may differ from a plain program's by a relative error of at most 0.0049.
Values may be sent and summed in bfloat16 or wider, within the bound.
No kernel may reach another device: no remote copies, remote signals or barrier semaphores. Data moves between devices by JAX's collectives and lax.ppermute only.
A program may use at most 128 MiB of HBM per device.

v0:
```python
import math
import jax
import jax.numpy as jnp
import numpy as np
from jax import lax
from jax.sharding import PartitionSpec as P

BLADES = 22


def twiddles(row_count, col_count, modulus):
    rows_iota = jnp.arange(row_count, dtype=jnp.int32)[:, None]
    cols_iota = jnp.arange(col_count, dtype=jnp.int32)[None, :]
    phase = rows_iota * cols_iota % modulus
    angle = phase.astype(jnp.float32) * (2.0 * math.pi / modulus)
    return (jnp.cos(angle), jnp.sin(angle))


def real_form(jac_item):
    jac_real = jac_item[:, 0]
    jac_imag = jac_item[:, 1]
    upper = jnp.concatenate([jac_real, -jac_imag], axis=2)
    lower = jnp.concatenate([jac_imag, jac_real], axis=2)
    return jnp.concatenate([upper, lower], axis=1)


def shards(field, jacobian, coupling):
    local_stations, axial_count, freq_count, full_width = field.shape
    node_count = lax.axis_size("azim")
    item_count = axial_count * freq_count
    per_device = item_count // node_count
    half_width = full_width // 2
    order_count = jacobian.shape[0]
    precise = lax.Precision.HIGH
    flattened = field.reshape(local_stations, item_count, full_width)
    columns = lax.all_to_all(flattened, "azim", split_axis=1, concat_axis=0, tiled=True)
    targets = np.arange(node_count * per_device) % freq_count
    outgoing = jnp.take(jacobian, jnp.asarray(targets, dtype=jnp.int32), axis=1)
    local_jac = lax.all_to_all(outgoing, "azim", split_axis=1, concat_axis=3, tiled=True)
    stations = columns.shape[0]
    passage = stations // BLADES
    norm_scale = 1.0 / math.sqrt(stations)
    cos_blade, sin_blade = twiddles(BLADES, BLADES, BLADES)
    cos_twist, sin_twist = twiddles(BLADES, passage, stations)
    cos_pass, sin_pass = twiddles(passage, passage, passage)
    twist_c = cos_twist[:, :, None]
    twist_s = sin_twist[:, :, None]
    gate_table = coupling.astype(jnp.bfloat16)

    def transform(position, buffer):
        sample = lax.dynamic_index_in_dim(columns, position, 1, keepdims=False)
        values = sample.astype(jnp.float32).reshape(BLADES, passage, full_width)
        first_c = jnp.einsum("rb,bav->rav", cos_blade, values, precision=precise)
        first_s = jnp.einsum("rb,bav->rav", sin_blade, values, precision=precise)
        part_real = first_c[..., :half_width] + first_s[..., half_width:]
        part_imag = first_c[..., half_width:] - first_s[..., :half_width]
        turned = jnp.concatenate(
            [twist_c * part_real + twist_s * part_imag, twist_c * part_imag - twist_s * part_real],
            axis=-1,
        )
        second_c = jnp.einsum("qa,rav->qrv", cos_pass, turned, precision=precise)
        second_s = jnp.einsum("qa,rav->qrv", sin_pass, turned, precision=precise)
        modes = (
            jnp.concatenate(
                [
                    second_c[..., :half_width] + second_s[..., half_width:],
                    second_c[..., half_width:] - second_s[..., :half_width],
                ],
                axis=-1,
            )
            * norm_scale
        ).astype(jnp.bfloat16)
        operator = real_form(lax.dynamic_index_in_dim(local_jac, position, 1, keepdims=False))
        coupled = jnp.zeros((passage, BLADES, full_width), jnp.float32)
        for order_idx in range(order_count):
            moved = (
                jnp.roll(modes, -(order_idx - order_count // 2), axis=0)
                * gate_table[:, order_idx][:, None, None]
            )
            coupled = coupled + jnp.einsum(
                "qri,oi->qro", moved, operator[order_idx], preferred_element_type=jnp.float32
            )
        third_c = jnp.einsum("qa,qrv->rav", cos_pass, coupled, precision=precise)
        third_s = jnp.einsum("qa,qrv->rav", sin_pass, coupled, precision=precise)
        back_real = third_c[..., :half_width] - third_s[..., half_width:]
        back_imag = third_c[..., half_width:] + third_s[..., :half_width]
        spun = jnp.concatenate(
            [twist_c * back_real - twist_s * back_imag, twist_c * back_imag + twist_s * back_real],
            axis=-1,
        )
        last_c = jnp.einsum("rb,rav->bav", cos_blade, spun, precision=precise)
        last_s = jnp.einsum("rb,rav->bav", sin_blade, spun, precision=precise)
        restored = (
            jnp.concatenate(
                [
                    last_c[..., :half_width] - last_s[..., half_width:],
                    last_c[..., half_width:] + last_s[..., :half_width],
                ],
                axis=-1,
            )
            * norm_scale
        )
        result = restored.reshape(stations, full_width).astype(jnp.bfloat16)
        return lax.dynamic_update_index_in_dim(buffer, result, position, 1)

    initial = jnp.zeros((stations, per_device, full_width), jnp.bfloat16)
    finished = lax.fori_loop(0, per_device, transform, initial)
    returned = lax.all_to_all(finished, "azim", split_axis=0, concat_axis=1, tiled=True)
    return returned.reshape(local_stations, axial_count, freq_count, full_width)


def solution(mesh):
    placed = (P(("group", "azim"), None, None, None), P(None, None, None, "azim", None), P())
    return jax.shard_map(
        shards,
        mesh=mesh,
        in_specs=placed,
        out_specs=P(("group", "azim"), None, None, None),
        check_vma=False,
    )
```

profile of v0, /device:TPU:1, one launch (start us, length us, event | category | flops | bytes accessed | tf_op | source)
XLA Modules:
  0.0 432.2 jit_solution(5272978858724558747)
XLA Ops:
  0.0 3.9 copy.112
  3.9 7.5 %all-to-all-start = ((bf16[22,64,640]{2,0,1:T(8,128)(2,1)}), bf16[22,64,640]{2,0,1:T(8,128)(2,1)S(1)}, u32[]{:S(2)}, u32[]{:S(2)}) async-start(bf16[22,64,640]{2,0,1:T(8,128)(2,1)} %bitcast.173), calls=%async_computation | async-start | bytes 3932160 | tf_op jit(solution)/shard_map/all_to_all | solution.py:36
  11.4 21.1 %gather_fusion = bf16[64,5,2,20,320]{4,2,3,1,0:T(2,128)(2,1)} fusion(bf16[5,8,2,20,320]{4,2,3,1,0:T(2,128)(2,1)S(1)} %copy-done, s32[1024]{0:T(1024)S(1)} %pad_clamp_fusion), kind=kCustom, calls=%fused_computation | custom fusion | bytes 16384256 | tf_op jit(solution)/shard_map/jit(_take)/gather | solution.py:38
  32.6 18.0 %all-to-all-done = bf16[22,64,640]{2,0,1:T(8,128)(2,1)S(1)} async-done(((bf16[22,64,640]{2,0,1:T(8,128)(2,1)}), bf16[22,64,640]{2,0,1:T(8,128)(2,1)S(1)}, u32[]{:S(2)}, u32[]{:S(2)}) %all-to-all-start) | async-done | bytes 1802272 | tf_op jit(solution)/shard_map/all_to_all | solution.py:36
  50.6 10.5 %all-to-all-start.1 = ((bf16[5,64,2,20,320]{4,2,3,0,1:T(2,128)(2,1)}), bf16[5,64,2,20,320]{4,2,3,0,1:T(2,128)(2,1)}, u32[]{:S(2)}, u32[]{:S(2)}) async-start(bf16[5,64,2,20,320]{4,2,3,0,1:T(2,128)(2,1)} %bitcast.171), calls=%async_computation.1 | async-start | bytes 19660800 | tf_op jit(solution)/shard_map/all_to_all | solution.py:39
  61.1 0.7 copy.125
  62.0 175.3 %all-to-all-done.1 = bf16[5,64,2,20,320]{4,2,3,0,1:T(2,128)(2,1)} async-done(((bf16[5,64,2,20,320]{4,2,3,0,1:T(2,128)(2,1)}), bf16[5,64,2,20,320]{4,2,3,0,1:T(2,128)(2,1)}, u32[]{:S(2)}, u32[]{:S(2)}) %all-to-all-start.1) | async-done | bytes 8192032 | tf_op jit(solution)/shard_map/all_to_all | solution.py:39
  237.3 9.3 %copy.115 = bf16[5,16,4,2,20,320]{5,3,4,1,2,0:T(2,128)(2,1)} copy(bf16[5,16,4,2,20,320]{5,3,4,0,2,1:T(2,128)(2,1)} %bitcast.6) | data formatting | bytes 16384000 | tf_op jit(solution)/shard_map/all_to_all | solution.py:39
  246.5 96.6 %while.15 = (s32[]{:T(128)}, bf16[352,4,640]{2,0,1:T(8,128)(2,1)}, bf16[352,4,640]{2,0,1:T(8,128)(2,1)S(1)}, bf16[16,5]{0,1:T(8,128)(2,1)S(1)}, bf16[5,4,2,320,320]{4,2,3,1,0:T(2,128)(2,1)}, /*index=5*/s32[]{:T(128)}) while((s32[]{:T(128)}, bf16[352,4,640]{2,0,1:T(8,128)(2,1)}, bf16[352,4,640]{2,0,1:T(8,128)(2,1)S(1)}, ...), condition=%wide.region_1.2_spmd.clone.clone, body=%wide.region_0.1_spmd.clone.clone.sunk | while | flops 1674994944 | bytes 79102776 | solution.py:107
  246.7 3.4 constant_dynamic-slice_fusion.4
  250.8 6.1 %maximum_maximum_fusion.2 = bf16[5,640,640]{2,1,0:T(8,128)(2,1)S(1)} fusion(bf16[5,320,320]{2,1,0:T(8,128)(2,1)S(1)} %get-tuple-element.401, bf16[5,320,320]{2,1,0:T(8,128)(2,1)S(1)} %get-tuple-element.402, bf16[5,320,320]{2,1,0:T(8,128)(2,1)S(1)} %fusion.160), kind=kLoop, calls=%fused_computation.7.clone.1 | loop fusion | flops 16384000 | bytes 7168000 | tf_op jit(solution)/shard_map/while/body/eval_jaxpr/concatenate | solution.py:24
  258.8 0.6 convolution_bitcast_fusion.14
  259.4 0.6 convolution_bitcast_fusion.15
  261.7 0.7 fusion.165
  262.3 0.7 convolution_add_fusion.8
  263.0 0.7 convolution_add_fusion.9
  264.1 0.7 convolution_add_fusion.10
  264.8 0.7 convolution_add_fusion.11
  265.5 0.6 fusion.166
  267.7 0.7 convolution_bitcast_fusion.16
  268.4 0.7 convolution_bitcast_fusion.17
  269.7 1.0 fusion.168
  270.8 3.4 constant_dynamic-slice_fusion.4
  274.9 6.1 %maximum_maximum_fusion.2 = bf16[5,640,640]{2,1,0:T(8,128)(2,1)S(1)} fusion(bf16[5,320,320]{2,1,0:T(8,128)(2,1)S(1)} %get-tuple-element.401, bf16[5,320,320]{2,1,0:T(8,128)(2,1)S(1)} %get-tuple-element.402, bf16[5,320,320]{2,1,0:T(8,128)(2,1)S(1)} %fusion.160), kind=kLoop, calls=%fused_computation.7.clone.1 | loop fusion | flops 16384000 | bytes 7168000 | tf_op jit(solution)/shard_map/while/body/eval_jaxpr/concatenate | solution.py:24
  282.9 0.6 convolution_bitcast_fusion.14
  283.5 0.6 convolution_bitcast_fusion.15
  285.8 0.7 fusion.165
  286.5 0.7 convolution_add_fusion.8
  287.2 0.7 convolution_add_fusion.9
  288.3 0.7 convolution_add_fusion.10
  288.9 0.7 convolution_add_fusion.11
  289.6 0.6 fusion.166
  291.9 0.7 convolution_bitcast_fusion.16
  292.6 0.7 convolution_bitcast_fusion.17
  293.9 1.0 fusion.168
  295.0 3.4 constant_dynamic-slice_fusion.4
  299.1 6.1 %maximum_maximum_fusion.2 = bf16[5,640,640]{2,1,0:T(8,128)(2,1)S(1)} fusion(bf16[5,320,320]{2,1,0:T(8,128)(2,1)S(1)} %get-tuple-element.401, bf16[5,320,320]{2,1,0:T(8,128)(2,1)S(1)} %get-tuple-element.402, bf16[5,320,320]{2,1,0:T(8,128)(2,1)S(1)} %fusion.160), kind=kLoop, calls=%fused_computation.7.clone.1 | loop fusion | flops 16384000 | bytes 7168000 | tf_op jit(solution)/shard_map/while/body/eval_jaxpr/concatenate | solution.py:24
  307.1 0.6 convolution_bitcast_fusion.14
  307.7 0.6 convolution_bitcast_fusion.15
  310.0 0.7 fusion.165
  310.6 0.7 convolution_add_fusion.8
  311.3 0.7 convolution_add_fusion.9
  312.4 0.7 convolution_add_fusion.10
  313.1 0.7 convolution_add_fusion.11
  313.8 0.6 fusion.166
  316.0 0.7 convolution_bitcast_fusion.16
  316.7 0.7 convolution_bitcast_fusion.17
  318.0 1.0 fusion.168
  319.1 3.4 constant_dynamic-slice_fusion.4
  323.2 6.1 %maximum_maximum_fusion.2 = bf16[5,640,640]{2,1,0:T(8,128)(2,1)S(1)} fusion(bf16[5,320,320]{2,1,0:T(8,128)(2,1)S(1)} %get-tuple-element.401, bf16[5,320,320]{2,1,0:T(8,128)(2,1)S(1)} %get-tuple-element.402, bf16[5,320,320]{2,1,0:T(8,128)(2,1)S(1)} %fusion.160), kind=kLoop, calls=%fused_computation.7.clone.1 | loop fusion | flops 16384000 | bytes 7168000 | tf_op jit(solution)/shard_map/while/body/eval_jaxpr/concatenate | solution.py:24
  331.2 0.6 convolution_bitcast_fusion.14
  331.8 0.6 convolution_bitcast_fusion.15
  334.1 0.7 fusion.165
  334.8 0.7 convolution_add_fusion.8
  335.5 0.7 convolution_add_fusion.9
  336.6 0.7 convolution_add_fusion.10
  337.2 0.7 convolution_add_fusion.11
  340.2 0.7 convolution_bitcast_fusion.16
  340.9 0.7 convolution_bitcast_fusion.17
  342.2 1.0 fusion.168
  343.1 2.4 copy.118
  345.6 84.3 %all_to_all.51 = bf16[352,4,640]{2,1,0:T(4,128)(2,1)S(1)} all-to-all(bf16[352,4,640]{2,1,0:T(4,128)(2,1)S(1)} %copy.118), channel_id=1, replica_groups=mesh['group'=2,'azim'=16] {'azim'}, dimensions={0} | all-to-all | bytes 3604480 | tf_op jit(solution)/shard_map/all_to_all | solution.py:108
  429.8 0.9 copy.119
  430.7 1.4 reshape.120
  (117 shorter events, 28.5 us)
Async XLA Ops:
  0.0 11.4 %copy-start = (bf16[5,8,2,20,320]{4,2,3,1,0:T(2,128)(2,1)S(1)}, bf16[5,8,2,20,320]{4,2,3,1,0:T(2,128)(2,1)}, u32[]{:S(2)}) copy-start(bf16[5,8,2,20,320]{4,2,3,1,0:T(2,128)(2,1)} %param.7) | copy-start | bytes 3072004
  3.9 7.5 %copy-start.3 = (s32[64]{0:T(128)S(1)}, s32[64]{0:T(128)}, u32[]{:S(2)}) copy-start(s32[64]{0:T(128)} %constant.113) | copy-start | bytes 772
  3.9 46.7 %all-to-all-start = ((bf16[22,64,640]{2,0,1:T(8,128)(2,1)}), bf16[22,64,640]{2,0,1:T(8,128)(2,1)S(1)}, u32[]{:S(2)}, u32[]{:S(2)}) async-start(bf16[22,64,640]{2,0,1:T(8,128)(2,1)} %bitcast.173), calls=%async_computation | async-start | bytes 3932160 | tf_op jit(solution)/shard_map/all_to_all | solution.py:36
  50.6 10.5 %copy-start.2 = (s32[16,5]{0,1:T(8,128)S(1)}, s32[16,5]{0,1:T(8,128)}, u32[]{:S(2)}) copy-start(s32[16,5]{0,1:T(8,128)} %param.8) | copy-start | bytes 964
  50.6 186.7 %all-to-all-start.1 = ((bf16[5,64,2,20,320]{4,2,3,0,1:T(2,128)(2,1)}), bf16[5,64,2,20,320]{4,2,3,0,1:T(2,128)(2,1)}, u32[]{:S(2)}, u32[]{:S(2)}) async-start(bf16[5,64,2,20,320]{4,2,3,0,1:T(2,128)(2,1)} %bitcast.171), calls=%async_computation.1 | async-start | bytes 19660800 | tf_op jit(solution)/shard_map/all_to_all | solution.py:39
  429.8 2.3 copy-start.1
where the time goes:
time: 433 us; the launch traced here: 432 us
  waiting for transfers between devices  193 us (45%)
  blocking collectives  84.3 us (19%)
  local copies, waits for them, and re-layouts  61.2 us (14%)
  other arithmetic  41.7 us (10%)
  matrix products  32.7 us (8%)
  starting transfers between devices  17.9 us (4%)
    all_to_all x1, waiting for transfers between devices, shards(): lax.all_to_all(outgoing, 'azim', split_axis=1, concat_axis=3, tiled=True)  175 us
    all_to_all x1, blocking collectives, shards(): lax.all_to_all(finished, 'azim', split_axis=0, concat_axis=1, tiled=True)  84.3 us
    concatenate x4, other arithmetic, real_form(): return jnp.concatenate([upper, lower], axis=1)  24.3 us
    gather x1, local copies, waits for them, and re-layouts, shards(): outgoing = jnp.take(jacobian, jnp.asarray(targets, dtype=jnp.int32), axis=1)  21.1 us
    all_to_all x1, waiting for transfers between devices, shards(): lax.all_to_all(flattened, 'azim', split_axis=1, concat_axis=0, tiled=True)  18 us
    dynamic_slice x8, local copies, waits for them, and re-layouts, transform(): lax.dynamic_index_in_dim(local_jac, position, 1, keepdims=False)  15 us
    dot_general x20, matrix products, transform(): jnp.einsum('qri,oi->qro', moved, operator[order_idx], preferred_element_t...  13.5 us
    all_to_all x1, starting transfers between devices, shards(): lax.all_to_all(outgoing, 'azim', split_axis=1, concat_axis=3, tiled=True)  10.5 us
  transfers between devices with their start and end apart: 2, of which 2 were waited for; matrix products, arithmetic and copies ran while one was open for 5% of the time, Pallas kernels for 0%

commit v1 on v0

--- a/solution.py
+++ b/solution.py
@@ -6,6 +6,30 @@
 from jax.sharding import PartitionSpec as P
 
 BLADES = 22
+
+
+def cut_along(value, dim, size):
+    dims = value.shape
+    tiles = value.reshape(*dims[:dim], size, dims[dim] // size, *dims[dim + 1 :])
+    return jnp.moveaxis(tiles, dim, 0)
+
+
+def in_order(pieces, dim):
+    pieces = jnp.moveaxis(pieces, 0, dim)
+    lengths = pieces.shape
+    return pieces.reshape(*lengths[:dim], lengths[dim] * lengths[dim + 1], *lengths[dim + 2 :])
+
+
+def rotated_exchange(x, axis, split_dim, concat_dim):
+    count, index = (lax.axis_size(axis), lax.axis_index(axis))
+    tiles = cut_along(x, split_dim, count)
+    out = tiles
+    for step in range(1, count):
+        target, source = ((index + step) % count, (index - step) % count)
+        sent = lax.dynamic_index_in_dim(tiles, target, 0)
+        other = lax.ppermute(sent, axis, [(i, (i + step) % count) for i in range(count)])
+        out = lax.dynamic_update_slice_in_dim(out, other, source, axis=0)
+    return in_order(out, concat_dim)
 
 
 def twiddles(row_count, col_count, modulus):
@@ -105,7 +129,7 @@
 
     initial = jnp.zeros((stations, per_device, full_width), jnp.bfloat16)
     finished = lax.fori_loop(0, per_device, transform, initial)
-    returned = lax.all_to_all(finished, "azim", split_axis=0, concat_axis=1, tiled=True)
+    returned = rotated_exchange(finished, "azim", 0, 1)
     return returned.reshape(local_stations, axial_count, freq_count, full_width)
 
 

time: 433 us -> 442 us (1.021)
  blocking collectives: 84.3 us -> 0 us
  starting transfers between devices: 17.9 us -> 98.4 us
  waiting for transfers between devices: 193 us -> 200 us
  local copies, waits for them, and re-layouts: 61.2 us -> 67.2 us
    all_to_all x1 -> x0, blocking collectives: 84.3 us -> none  [shards(): lax.all_to_all(finished, 'azim', split_axis=0, concat_axis=1, tiled=True)]
    ppermute x0 -> x15, starting transfers between devices: none -> 80.4 us  [rotated_exchange(): lax.ppermute(sent, axis, [(i, (i + step) % count) for i in range(count)])]
    ppermute x0 -> x15, waiting for transfers between devices: none -> 6.58 us  [rotated_exchange(): lax.ppermute(sent, axis, [(i, (i + step) % count) for i in range(count)])]
  transfers between devices with their start and end apart: 2 -> 17, of which waited for: 2 -> 7; matrix products, arithmetic and copies ran while one was open for 5% -> 5% of each run, Pallas kernels for 0% -> 0%
where the time goes in v1:
time: 442 us; the launch traced here: 441 us
  waiting for transfers between devices  200 us (45%)
  starting transfers between devices  98.4 us (22%)
  local copies, waits for them, and re-layouts  67.2 us (15%)
  other arithmetic  41.7 us (9%)
  matrix products  32.7 us (7%)
    all_to_all x1, waiting for transfers between devices, shards(): lax.all_to_all(outgoing, 'azim', split_axis=1, concat_axis=3, tiled=True)  175 us
    ppermute x15, starting transfers between devices, rotated_exchange(): lax.ppermute(sent, axis, [(i, (i + step) % count) for i in range(count)])  80.4 us
    concatenate x4, other arithmetic, real_form(): return jnp.concatenate([upper, lower], axis=1)  24.3 us
    gather x1, local copies, waits for them, and re-layouts, shards(): outgoing = jnp.take(jacobian, jnp.asarray(targets, dtype=jnp.int32), axis=1)  21.1 us
    all_to_all x1, waiting for transfers between devices, shards(): lax.all_to_all(flattened, 'azim', split_axis=1, concat_axis=0, tiled=True)  18 us
    dynamic_slice x8, local copies, waits for them, and re-layouts, transform(): lax.dynamic_index_in_dim(local_jac, position, 1, keepdims=False)  15 us
    dot_general x20, matrix products, transform(): jnp.einsum('qri,oi->qro', moved, operator[order_idx], preferred_element_t...  13.5 us
    all_to_all x1, starting transfers between devices, shards(): lax.all_to_all(outgoing, 'azim', split_axis=1, concat_axis=3, tiled=True)  10.5 us
  transfers between devices with their start and end apart: 17, of which 7 were waited for; matrix products, arithmetic and copies ran while one was open for 5% of the time, Pallas kernels for 0%

profile of v1, /device:TPU:1, one launch (start us, length us, event | category | flops | bytes accessed | tf_op | source)
XLA Modules:
  0.0 441.0 jit_solution(17199434742388690631)
XLA Ops:
  0.0 3.9 copy.142
  3.9 7.5 %all-to-all-start = ((bf16[22,64,640]{2,0,1:T(8,128)(2,1)}), bf16[22,64,640]{2,0,1:T(8,128)(2,1)S(1)}, u32[]{:S(2)}, u32[]{:S(2)}) async-start(bf16[22,64,640]{2,0,1:T(8,128)(2,1)} %bitcast.175), calls=%async_computation | async-start | bytes 3932160 | tf_op jit(solution)/shard_map/all_to_all | solution.py:60
  11.4 21.1 %gather_fusion = bf16[64,5,2,20,320]{4,2,3,1,0:T(2,128)(2,1)} fusion(bf16[5,8,2,20,320]{4,2,3,1,0:T(2,128)(2,1)S(1)} %copy-done, s32[1024]{0:T(1024)S(1)} %pad_clamp_fusion), kind=kCustom, calls=%fused_computation | custom fusion | bytes 16384256 | tf_op jit(solution)/shard_map/jit(_take)/gather | solution.py:62
  32.5 18.0 %all-to-all-done = bf16[22,64,640]{2,0,1:T(8,128)(2,1)S(1)} async-done(((bf16[22,64,640]{2,0,1:T(8,128)(2,1)}), bf16[22,64,640]{2,0,1:T(8,128)(2,1)S(1)}, u32[]{:S(2)}, u32[]{:S(2)}) %all-to-all-start) | async-done | bytes 1802272 | tf_op jit(solution)/shard_map/all_to_all | solution.py:60
  50.5 10.5 %all-to-all-start.1 = ((bf16[5,64,2,20,320]{4,2,3,0,1:T(2,128)(2,1)}), bf16[5,64,2,20,320]{4,2,3,0,1:T(2,128)(2,1)}, u32[]{:S(2)}, u32[]{:S(2)}) async-start(bf16[5,64,2,20,320]{4,2,3,0,1:T(2,128)(2,1)} %bitcast.170), calls=%async_computation.1 | async-start | bytes 19660800 | tf_op jit(solution)/shard_map/all_to_all | solution.py:63
  61.1 0.7 copy.155
  62.0 175.2 %all-to-all-done.1 = bf16[5,64,2,20,320]{4,2,3,0,1:T(2,128)(2,1)} async-done(((bf16[5,64,2,20,320]{4,2,3,0,1:T(2,128)(2,1)}), bf16[5,64,2,20,320]{4,2,3,0,1:T(2,128)(2,1)}, u32[]{:S(2)}, u32[]{:S(2)}) %all-to-all-start.1) | async-done | bytes 8192032 | tf_op jit(solution)/shard_map/all_to_all | solution.py:63
  237.2 9.2 %copy.145 = bf16[5,16,4,2,20,320]{5,3,4,1,2,0:T(2,128)(2,1)} copy(bf16[5,16,4,2,20,320]{5,3,4,0,2,1:T(2,128)(2,1)} %bitcast.6) | data formatting | bytes 16384000 | tf_op jit(solution)/shard_map/all_to_all | solution.py:63
  246.5 96.6 %while.15 = (s32[]{:T(128)}, bf16[352,4,640]{2,0,1:T(8,128)(2,1)}, bf16[352,4,640]{2,0,1:T(8,128)(2,1)S(1)}, bf16[16,5]{0,1:T(8,128)(2,1)S(1)}, bf16[5,4,2,320,320]{4,2,3,1,0:T(2,128)(2,1)}, /*index=5*/s32[]{:T(128)}) while((s32[]{:T(128)}, bf16[352,4,640]{2,0,1:T(8,128)(2,1)}, bf16[352,4,640]{2,0,1:T(8,128)(2,1)S(1)}, ...), condition=%wide.region_1.2_spmd.clone.clone, body=%wide.region_0.1_spmd.clone.clone.sunk | while | flops 1674994944 | bytes 79102776 | solution.py:131
  246.6 3.4 constant_dynamic-slice_fusion.19
  250.7 6.1 %maximum_maximum_fusion.2 = bf16[5,640,640]{2,1,0:T(8,128)(2,1)S(1)} fusion(bf16[5,320,320]{2,1,0:T(8,128)(2,1)S(1)} %get-tuple-element.416, bf16[5,320,320]{2,1,0:T(8,128)(2,1)S(1)} %get-tuple-element.417, bf16[5,320,320]{2,1,0:T(8,128)(2,1)S(1)} %fusion.160), kind=kLoop, calls=%fused_computation.7.clone.1 | loop fusion | flops 16384000 | bytes 7168000 | tf_op jit(solution)/shard_map/while/body/eval_jaxpr/concatenate | solution.py:48
  261.6 0.7 fusion.165
  262.3 0.7 convolution_add_fusion.8
  263.0 0.7 convolution_add_fusion.9
  264.1 0.7 convolution_add_fusion.10
  264.7 0.7 convolution_add_fusion.11
  267.7 0.7 convolution_bitcast_fusion.16
  268.4 0.7 convolution_bitcast_fusion.17
  269.7 1.0 fusion.168
  270.8 3.4 constant_dynamic-slice_fusion.19
  274.9 6.1 %maximum_maximum_fusion.2 = bf16[5,640,640]{2,1,0:T(8,128)(2,1)S(1)} fusion(bf16[5,320,320]{2,1,0:T(8,128)(2,1)S(1)} %get-tuple-element.416, bf16[5,320,320]{2,1,0:T(8,128)(2,1)S(1)} %get-tuple-element.417, bf16[5,320,320]{2,1,0:T(8,128)(2,1)S(1)} %fusion.160), kind=kLoop, calls=%fused_computation.7.clone.1 | loop fusion | flops 16384000 | bytes 7168000 | tf_op jit(solution)/shard_map/while/body/eval_jaxpr/concatenate | solution.py:48
  285.8 0.7 fusion.165
  287.1 0.7 convolution_add_fusion.9
  288.9 0.7 convolution_add_fusion.11
  291.8 0.7 convolution_bitcast_fusion.16
  292.5 0.7 convolution_bitcast_fusion.17
  293.8 1.0 fusion.168
  294.9 3.4 constant_dynamic-slice_fusion.19
  299.0 6.1 %maximum_maximum_fusion.2 = bf16[5,640,640]{2,1,0:T(8,128)(2,1)S(1)} fusion(bf16[5,320,320]{2,1,0:T(8,128)(2,1)S(1)} %get-tuple-element.416, bf16[5,320,320]{2,1,0:T(8,128)(2,1)S(1)} %get-tuple-element.417, bf16[5,320,320]{2,1,0:T(8,128)(2,1)S(1)} %fusion.160), kind=kLoop, calls=%fused_computation.7.clone.1 | loop fusion | flops 16384000 | bytes 7168000 | tf_op jit(solution)/shard_map/while/body/eval_jaxpr/concatenate | solution.py:48
  309.9 0.7 fusion.165
  311.3 0.7 convolution_add_fusion.9
  313.0 0.7 convolution_add_fusion.11
  316.0 0.7 convolution_bitcast_fusion.16
  316.7 0.7 convolution_bitcast_fusion.17
  318.0 1.0 fusion.168
  319.1 3.4 constant_dynamic-slice_fusion.19
  323.2 6.1 %maximum_maximum_fusion.2 = bf16[5,640,640]{2,1,0:T(8,128)(2,1)S(1)} fusion(bf16[5,320,320]{2,1,0:T(8,128)(2,1)S(1)} %get-tuple-element.416, bf16[5,320,320]{2,1,0:T(8,128)(2,1)S(1)} %get-tuple-element.417, bf16[5,320,320]{2,1,0:T(8,128)(2,1)S(1)} %fusion.160), kind=kLoop, calls=%fused_computation.7.clone.1 | loop fusion | flops 16384000 | bytes 7168000 | tf_op jit(solution)/shard_map/while/body/eval_jaxpr/concatenate | solution.py:48
  334.1 0.7 fusion.165
  335.4 0.7 convolution_add_fusion.9
  337.2 0.7 convolution_add_fusion.11
  340.1 0.7 convolution_bitcast_fusion.16
  340.8 0.7 convolution_bitcast_fusion.17
  342.1 1.0 fusion.168
  343.1 2.4 copy.148
  345.6 13.2 %collective-permute-start = (bf16[1,22,4,640]{3,2,1,0:T(4,128)(2,1)S(1)}, bf16[1,22,4,640]{3,2,1,0:T(4,128)(2,1)S(1)}, u32[]{:S(2)}, u32[]{:S(2)}) collective-permute-start(bf16[1,22,4,640]{3,2,1,0:T(4,128)(2,1)S(1)} %constant_dynamic-slice_fusion.16), channel_id=1, source_target_pairs={{0,1},{1,2},{2,3},{3,4},{4,5},{5,6},{6,7},{7,8},{8,9},{9,10},{10,1... | collective-permute-start | bytes 337928 | tf_op jit(solution)/shard_map/ppermute | solution.py:30
  358.7 1.8 collective-permute-done
  360.5 1.4 constant_dynamic-slice_fusion.2
  362.0 25.1 %collective-permute-start.1 = (bf16[1,22,4,640]{3,2,1,0:T(4,128)(2,1)S(1)}, bf16[1,22,4,640]{3,2,1,0:T(4,128)(2,1)S(1)}, u32[]{:S(2)}, u32[]{:S(2)}) collective-permute-start(bf16[1,22,4,640]{3,2,1,0:T(4,128)(2,1)S(1)} %get-tuple-element.354), channel_id=1, source_target_pairs={{0,2},{1,3},{2,4},{3,5},{4,6},{5,7},{6,8},{7,9},{8,10},{9,11},{10,... | collective-permute-start | bytes 337928 | tf_op jit(solution)/shard_map/ppermute | solution.py:30
  387.0 4.2 collective-permute-start.2
  391.2 1.0 collective-permute-start.3
  392.2 1.2 collective-permute-start.4
  393.4 1.6 collective-permute-start.5
  395.0 2.6 collective-permute-start.6
  397.7 0.9 collective-permute-done.2
  398.6 1.5 collective-permute-start.7
  400.2 2.7 collective-permute-start.8
  403.0 14.6 %collective-permute-start.9 = (bf16[1,22,4,640]{3,2,1,0:T(4,128)(2,1)S(1)}, bf16[1,22,4,640]{3,2,1,0:T(4,128)(2,1)S(1)}, u32[]{:S(2)}, u32[]{:S(2)}) collective-permute-start(bf16[1,22,4,640]{3,2,1,0:T(4,128)(2,1)S(1)} %get-tuple-element.346), channel_id=1, source_target_pairs={{0,10},{1,11},{2,12},{3,13},{4,14},{5,15},{6,0},{7,1},{8,2},{9,3},... | collective-permute-start | bytes 337928 | tf_op jit(solution)/shard_map/ppermute | solution.py:30
  417.6 4.7 %collective-permute-start.10 = (bf16[1,22,4,640]{3,2,1,0:T(4,128)(2,1)S(1)}, bf16[1,22,4,640]{3,2,1,0:T(4,128)(2,1)S(1)}, u32[]{:S(2)}, u32[]{:S(2)}) collective-permute-start(bf16[1,22,4,640]{3,2,1,0:T(4,128)(2,1)S(1)} %get-tuple-element.345), channel_id=1, source_target_pairs={{0,11},{1,12},{2,13},{3,14},{4,15},{5,0},{6,1},{7,2},{8,3},{9,4},{... | collective-permute-start | bytes 337928 | tf_op jit(solution)/shard_map/ppermute | solution.py:30
  422.4 4.5 %collective-permute-start.11 = (bf16[1,22,4,640]{3,2,1,0:T(4,128)(2,1)S(1)}, bf16[1,22,4,640]{3,2,1,0:T(4,128)(2,1)S(1)}, u32[]{:S(2)}, u32[]{:S(2)}) collective-permute-start(bf16[1,22,4,640]{3,2,1,0:T(4,128)(2,1)S(1)} %get-tuple-element.344), channel_id=1, source_target_pairs={{0,12},{1,13},{2,14},{3,15},{4,0},{5,1},{6,2},{7,3},{8,4},{9,5},{1... | collective-permute-start | bytes 337928 | tf_op jit(solution)/shard_map/ppermute | solution.py:30
  426.9 3.0 collective-permute-start.12
  430.9 1.3 collective-permute-done.12
  432.2 2.4 collective-permute-done.13
  434.9 2.2 copy.149
  437.1 3.9 reshape_reshape.3
  (162 shorter events, 40.9 us)
Async XLA Ops:
  0.0 11.4 %copy-start = (bf16[5,8,2,20,320]{4,2,3,1,0:T(2,128)(2,1)S(1)}, bf16[5,8,2,20,320]{4,2,3,1,0:T(2,128)(2,1)}, u32[]{:S(2)}) copy-start(bf16[5,8,2,20,320]{4,2,3,1,0:T(2,128)(2,1)} %param.7) | copy-start | bytes 3072004
  3.9 7.5 %copy-start.3 = (s32[64]{0:T(128)S(1)}, s32[64]{0:T(128)}, u32[]{:S(2)}) copy-start(s32[64]{0:T(128)} %constant.328) | copy-start | bytes 772
  3.9 46.7 %all-to-all-start = ((bf16[22,64,640]{2,0,1:T(8,128)(2,1)}), bf16[22,64,640]{2,0,1:T(8,128)(2,1)S(1)}, u32[]{:S(2)}, u32[]{:S(2)}) async-start(bf16[22,64,640]{2,0,1:T(8,128)(2,1)} %bitcast.175), calls=%async_computation | async-start | bytes 3932160 | tf_op jit(solution)/shard_map/all_to_all | solution.py:60
  50.5 10.5 %copy-start.2 = (s32[16,5]{0,1:T(8,128)S(1)}, s32[16,5]{0,1:T(8,128)}, u32[]{:S(2)}) copy-start(s32[16,5]{0,1:T(8,128)} %param.8) | copy-start | bytes 964
  50.5 186.7 %all-to-all-start.1 = ((bf16[5,64,2,20,320]{4,2,3,0,1:T(2,128)(2,1)}), bf16[5,64,2,20,320]{4,2,3,0,1:T(2,128)(2,1)}, u32[]{:S(2)}, u32[]{:S(2)}) async-start(bf16[5,64,2,20,320]{4,2,3,0,1:T(2,128)(2,1)} %bitcast.170), calls=%async_computation.1 | async-start | bytes 19660800 | tf_op jit(solution)/shard_map/all_to_all | solution.py:63
  345.6 14.9 %collective-permute-start = (bf16[1,22,4,640]{3,2,1,0:T(4,128)(2,1)S(1)}, bf16[1,22,4,640]{3,2,1,0:T(4,128)(2,1)S(1)}, u32[]{:S(2)}, u32[]{:S(2)}) collective-permute-start(bf16[1,22,4,640]{3,2,1,0:T(4,128)(2,1)S(1)} %constant_dynamic-slice_fusion.16), channel_id=1, source_target_pairs={{0,1},{1,2},{2,3},{3,4},{4,5},{5,6},{6,7},{7,8},{8,9},{9,10},{10,1... | collective-permute-start | bytes 337928 | tf_op jit(solution)/shard_map/ppermute | solution.py:30
  362.0 33.0 %collective-permute-start.1 = (bf16[1,22,4,640]{3,2,1,0:T(4,128)(2,1)S(1)}, bf16[1,22,4,640]{3,2,1,0:T(4,128)(2,1)S(1)}, u32[]{:S(2)}, u32[]{:S(2)}) collective-permute-start(bf16[1,22,4,640]{3,2,1,0:T(4,128)(2,1)S(1)} %get-tuple-element.354), channel_id=1, source_target_pairs={{0,2},{1,3},{2,4},{3,5},{4,6},{5,7},{6,8},{7,9},{8,10},{9,11},{10,... | collective-permute-start | bytes 337928 | tf_op jit(solution)/shard_map/ppermute | solution.py:30
  387.0 11.6 %collective-permute-start.2 = (bf16[1,22,4,640]{3,2,1,0:T(4,128)(2,1)S(1)}, bf16[1,22,4,640]{3,2,1,0:T(4,128)(2,1)S(1)}, u32[]{:S(2)}, u32[]{:S(2)}) collective-permute-start(bf16[1,22,4,640]{3,2,1,0:T(4,128)(2,1)S(1)} %get-tuple-element.353), channel_id=1, source_target_pairs={{0,3},{1,4},{2,5},{3,6},{4,7},{5,8},{6,9},{7,10},{8,11},{9,12},{10... | collective-permute-start | bytes 337928 | tf_op jit(solution)/shard_map/ppermute | solution.py:30
  391.2 9.0 %collective-permute-start.3 = (bf16[1,22,4,640]{3,2,1,0:T(4,128)(2,1)}, bf16[1,22,4,640]{3,2,1,0:T(4,128)(2,1)S(1)}, u32[]{:S(2)}, u32[]{:S(2)}) collective-permute-start(bf16[1,22,4,640]{3,2,1,0:T(4,128)(2,1)} %get-tuple-element.352), channel_id=1, source_target_pairs={{0,4},{1,5},{2,6},{3,7},{4,8},{5,9},{6,10},{7,11},{8,12},{9,13},{1... | collective-permute-start | bytes 337928 | tf_op jit(solution)/shard_map/ppermute | solution.py:30
  392.2 10.7 %collective-permute-start.4 = (bf16[1,22,4,640]{3,2,1,0:T(4,128)(2,1)}, bf16[1,22,4,640]{3,2,1,0:T(4,128)(2,1)S(1)}, u32[]{:S(2)}, u32[]{:S(2)}) collective-permute-start(bf16[1,22,4,640]{3,2,1,0:T(4,128)(2,1)} %get-tuple-element.351), channel_id=1, source_target_pairs={{0,5},{1,6},{2,7},{3,8},{4,9},{5,10},{6,11},{7,12},{8,13},{9,14},{... | collective-permute-start | bytes 337928 | tf_op jit(solution)/shard_map/ppermute | solution.py:30
  393.4 24.2 %collective-permute-start.5 = (bf16[1,22,4,640]{3,2,1,0:T(4,128)(2,1)}, bf16[1,22,4,640]{3,2,1,0:T(4,128)(2,1)S(1)}, u32[]{:S(2)}, u32[]{:S(2)}) collective-permute-start(bf16[1,22,4,640]{3,2,1,0:T(4,128)(2,1)} %get-tuple-element.350), channel_id=1, source_target_pairs={{0,6},{1,7},{2,8},{3,9},{4,10},{5,11},{6,12},{7,13},{8,14},{9,15},... | collective-permute-start | bytes 337928 | tf_op jit(solution)/shard_map/ppermute | solution.py:30
  395.0 27.4 %collective-permute-start.6 = (bf16[1,22,4,640]{3,2,1,0:T(4,128)(2,1)}, bf16[1,22,4,640]{3,2,1,0:T(4,128)(2,1)S(1)}, u32[]{:S(2)}, u32[]{:S(2)}) collective-permute-start(bf16[1,22,4,640]{3,2,1,0:T(4,128)(2,1)} %get-tuple-element.349), channel_id=1, source_target_pairs={{0,7},{1,8},{2,9},{3,10},{4,11},{5,12},{6,13},{7,14},{8,15},{9,0},... | collective-permute-start | bytes 337928 | tf_op jit(solution)/shard_map/ppermute | solution.py:30
  398.6 28.3 %collective-permute-start.7 = (bf16[1,22,4,640]{3,2,1,0:T(4,128)(2,1)}, bf16[1,22,4,640]{3,2,1,0:T(4,128)(2,1)S(1)}, u32[]{:S(2)}, u32[]{:S(2)}) collective-permute-start(bf16[1,22,4,640]{3,2,1,0:T(4,128)(2,1)} %get-tuple-element.348), channel_id=1, source_target_pairs={{0,8},{1,9},{2,10},{3,11},{4,12},{5,13},{6,14},{7,15},{8,0},{9,1},... | collective-permute-start | bytes 337928 | tf_op jit(solution)/shard_map/ppermute | solution.py:30
  400.2 29.7 %collective-permute-start.8 = (bf16[1,22,4,640]{3,2,1,0:T(4,128)(2,1)S(1)}, bf16[1,22,4,640]{3,2,1,0:T(4,128)(2,1)S(1)}, u32[]{:S(2)}, u32[]{:S(2)}) collective-permute-start(bf16[1,22,4,640]{3,2,1,0:T(4,128)(2,1)S(1)} %get-tuple-element.347), channel_id=1, source_target_pairs={{0,9},{1,10},{2,11},{3,12},{4,13},{5,14},{6,15},{7,0},{8,1},{9,2},... | collective-permute-start | bytes 337928 | tf_op jit(solution)/shard_map/ppermute | solution.py:30
  403.0 27.6 %collective-permute-start.9 = (bf16[1,22,4,640]{3,2,1,0:T(4,128)(2,1)S(1)}, bf16[1,22,4,640]{3,2,1,0:T(4,128)(2,1)S(1)}, u32[]{:S(2)}, u32[]{:S(2)}) collective-permute-start(bf16[1,22,4,640]{3,2,1,0:T(4,128)(2,1)S(1)} %get-tuple-element.346), channel_id=1, source_target_pairs={{0,10},{1,11},{2,12},{3,13},{4,14},{5,15},{6,0},{7,1},{8,2},{9,3},... | collective-permute-start | bytes 337928 | tf_op jit(solution)/shard_map/ppermute | solution.py:30
  417.6 13.1 %collective-permute-start.10 = (bf16[1,22,4,640]{3,2,1,0:T(4,128)(2,1)S(1)}, bf16[1,22,4,640]{3,2,1,0:T(4,128)(2,1)S(1)}, u32[]{:S(2)}, u32[]{:S(2)}) collective-permute-start(bf16[1,22,4,640]{3,2,1,0:T(4,128)(2,1)S(1)} %get-tuple-element.345), channel_id=1, source_target_pairs={{0,11},{1,12},{2,13},{3,14},{4,15},{5,0},{6,1},{7,2},{8,3},{9,4},{... | collective-permute-start | bytes 337928 | tf_op jit(solution)/shard_map/ppermute | solution.py:30
  422.4 8.4 %collective-permute-start.11 = (bf16[1,22,4,640]{3,2,1,0:T(4,128)(2,1)S(1)}, bf16[1,22,4,640]{3,2,1,0:T(4,128)(2,1)S(1)}, u32[]{:S(2)}, u32[]{:S(2)}) collective-permute-start(bf16[1,22,4,640]{3,2,1,0:T(4,128)(2,1)S(1)} %get-tuple-element.344), channel_id=1, source_target_pairs={{0,12},{1,13},{2,14},{3,15},{4,0},{5,1},{6,2},{7,3},{8,4},{9,5},{1... | collective-permute-start | bytes 337928 | tf_op jit(solution)/shard_map/ppermute | solution.py:30
  426.9 5.2 %collective-permute-start.12 = (bf16[1,22,4,640]{3,2,1,0:T(4,128)(2,1)S(1)}, bf16[1,22,4,640]{3,2,1,0:T(4,128)(2,1)S(1)}, u32[]{:S(2)}, u32[]{:S(2)}) collective-permute-start(bf16[1,22,4,640]{3,2,1,0:T(4,128)(2,1)S(1)} %get-tuple-element.343), channel_id=1, source_target_pairs={{0,13},{1,14},{2,15},{3,0},{4,1},{5,2},{6,3},{7,4},{8,5},{9,6},{10... | collective-permute-start | bytes 337928 | tf_op jit(solution)/shard_map/ppermute | solution.py:30
  430.0 4.6 %collective-permute-start.13 = (bf16[1,22,4,640]{3,2,1,0:T(4,128)(2,1)S(1)}, bf16[1,22,4,640]{3,2,1,0:T(4,128)(2,1)S(1)}, u32[]{:S(2)}, u32[]{:S(2)}) collective-permute-start(bf16[1,22,4,640]{3,2,1,0:T(4,128)(2,1)S(1)} %get-tuple-element.342), channel_id=1, source_target_pairs={{0,14},{1,15},{2,0},{3,1},{4,2},{5,3},{6,4},{7,5},{8,6},{9,7},{10,... | collective-permute-start | bytes 337928 | tf_op jit(solution)/shard_map/ppermute | solution.py:30
  430.6 4.2 collective-permute-start.14
  434.9 6.1 %copy-start.1 = (bf16[5,8,2,20,320]{4,2,3,1,0:T(2,128)(2,1)S(1)}, bf16[5,8,2,20,320]{4,2,3,1,0:T(2,128)(2,1)}, u32[]{:S(2)}) copy-start(bf16[5,8,2,20,320]{4,2,3,1,0:T(2,128)(2,1)} %param.7) | copy-start | bytes 3072004
